TPU v7x, 32 devices: a whole 2x2x4 slice. The times are simulated.
32 devices in a mesh: ep: 2 (over core), dp: 16 (over z, y, x).
Axes of the slice: x: 2, y: 2, z: 4, core: 2. Of those that a mesh axis runs over, the one named last changes fastest.
Arguments:
- tokens: bfloat16 [512, 7168], P('dp', 'ep'), may hold values from -6 to 6
- gate_weight: bfloat16 [16, 7168, 1024], P('dp', 'ep'), may hold values from -0.0625 to 0.0625
- up_weight: bfloat16 [16, 7168, 1024], P('dp', 'ep'), may hold values from -0.0625 to 0.0625
- down_weight: bfloat16 [16, 1024, 7168], P('dp', None, 'ep'), may hold values from -0.1875 to 0.1875
- targets: int32 [512, 8], P('dp'), may hold values from 0 to 15, all different within a row; in each aligned block of 32 rows (0 to 31, 32 to 63, ...) at most 32 rows name the same one
- mixing: float32 [512, 8], P('dp'), may hold values from 0.05 to 1
- move_plan: int32 [16], replicated, may hold values from 0 to 15, as said below
Outputs:
- mixed: bfloat16 [512, 7168], P('dp', 'ep')
Inputs may be any that keep to these rules, and one draw needn't show every extreme that they name: `targets`: each row names 8 different slots; within the 32 rows of one token group no slot is named more than 32 times, and in some groups one slot exactly 32 times. `move_plan`: every entry is either its own slot or one common source slot; the source serves its own copy; the slot after the source and the slot half of 16 after it (cyclically) always serve the source's copy, and each other slot does so with probability one half.
All inputs are finite; a program needn't handle non-finite values.
Results may differ from a plain program's by a relative error of at most 0.0058.
Values may be sent and summed in bfloat16 or wider, within the bound.
A program may use at most 128 MiB of HBM per device.

v0:
```python
import jax
import jax.numpy as jnp
from jax import lax
from jax.sharding import PartitionSpec as P


def spread(value, axis, source):
    kept = jnp.where(lax.axis_index(axis) == source, value, 0).astype(value.dtype)
    return lax.psum(kept, axis)


def run_expert(rows_in, gate_cols, up_cols, fetch_down):
    width = rows_in.shape[0]
    dims = (((0,), (1,)), ((), ()))
    gate_term = lax.dot_general(gate_cols, rows_in, dims, preferred_element_type=jnp.float32)
    up_term = lax.dot_general(up_cols, rows_in, dims, preferred_element_type=jnp.float32)
    summed = lax.psum_scatter(
        jnp.concatenate([gate_term, up_term], axis=1), "ep", scatter_dimension=0, tiled=True
    )
    hidden = (jax.nn.silu(summed[:, :width]) * summed[:, width:]).astype(jnp.bfloat16)
    down_rows = fetch_down()
    output = lax.dot_general(
        lax.all_gather(hidden, "ep", axis=0, tiled=True),
        down_rows,
        (((0,), (0,)), ((), ())),
        preferred_element_type=jnp.float32,
    )
    return output.astype(jnp.bfloat16)


def per_device(tokens, gate_weight, up_weight, down_weight, targets, mixing, move_plan):
    groups = lax.axis_size("dp")
    group_index = lax.axis_index("dp")
    token_rows = tokens.shape[0]
    per_token = targets.shape[1]
    slot_cap = min(token_rows, max(2, (2 * token_rows * per_token + groups - 1) // groups))
    slots = groups * slot_cap
    flat_targets = targets.reshape(-1)
    lanes = jnp.arange(groups, dtype=jnp.int32)
    hits = (flat_targets[:, None] == lanes[None, :]).astype(jnp.int32)
    earlier = jnp.cumsum(hits, axis=0) - hits
    position = jnp.sum(earlier * hits, axis=1)
    destination = flat_targets * slot_cap + position
    places = jnp.arange(slots, dtype=jnp.int32)
    matches = (
        destination.reshape(token_rows, per_token)[:, :, None] == places[None, None, :]
    ).astype(jnp.float32)
    pick_rows = jnp.sum(matches, axis=1).T.astype(jnp.bfloat16)
    outgoing = jnp.dot(pick_rows, tokens, preferred_element_type=jnp.float32).astype(jnp.bfloat16)
    arrived = lax.all_to_all(outgoing, "dp", split_axis=0, concat_axis=0, tiled=True)
    gate_cols = gate_weight[0]
    up_cols = up_weight[0]
    down_rows = down_weight[0]
    source_slot = jnp.max(jnp.where(move_plan != lanes, move_plan, -1))
    receives = move_plan[group_index] != group_index
    moved = spread(jnp.stack([gate_cols, up_cols]), "dp", source_slot)
    gate_cols = jnp.where(receives, moved[0], gate_cols)
    up_cols = jnp.where(receives, moved[1], up_cols)

    def fetch_down():
        moved_down = spread(down_rows, "dp", source_slot)
        return jnp.where(receives, moved_down, down_rows)

    results = run_expert(arrived, gate_cols, up_cols, fetch_down)
    returned = lax.all_to_all(results, "dp", split_axis=0, concat_axis=0, tiled=True)
    blend = jnp.sum(matches * mixing[:, :, None], axis=1)
    mixed = jnp.dot(blend, returned.astype(jnp.float32), precision=lax.Precision.HIGHEST)
    return mixed.astype(jnp.bfloat16)


def solution(mesh):
    return jax.shard_map(
        per_device,
        mesh=mesh,
        in_specs=(
            P("dp", "ep"),
            P("dp", "ep", None),
            P("dp", "ep", None),
            P("dp", None, "ep"),
            P("dp", None),
            P("dp", None),
            P(),
        ),
        out_specs=P("dp", "ep"),
        check_vma=False,
    )
```

profile of v0, /device:TPU:0, one launch (start us, length us, event | category | flops | bytes accessed | tf_op | source)
XLA Modules:
  0.0 842.2 jit_solution(5001722276564035526)
XLA Ops:
  6.5 1.3 fusion.17
  8.5 6.7 bitcast_select_fusion.1
  15.3 9.5 %maximum_select_fusion = bf16[2,3584,1024]{2,1,0:T(8,128)(2,1)} fusion(bf16[1,3584,1024]{2,1,0:T(8,128)(2,1)} %param.9, bf16[1,3584,1024]{2,1,0:T(8,128)(2,1)S(1)} %copy-done.2, pred[]{:T(512)S(6)} %eq.53), kind=kLoop, calls=%fused_computation | loop fusion | flops 14680064 | bytes 29360128 | tf_op jit(solution)/shard_map/jit(_where)/select_n | solution.py:8
  24.8 0.7 copy-done.3
  25.5 0.1 eq.46
  25.7 0.6 reduce-window.6
  26.3 0.2 slice_reduce_fusion
  26.5 0.1 fusion.15
  26.8 0.4 convert_reduce_fusion
  27.2 2.9 convolution_convert_fusion
  30.2 8.7 %all-to-all-start = ((bf16[16,32,3584]{2,1,0:T(8,128)(2,1)}), bf16[16,32,3584]{2,1,0:T(8,128)(2,1)}, u32[]{:S(2)}, u32[]{:S(2)}) async-start(bf16[16,32,3584]{2,1,0:T(8,128)(2,1)} %bitcast.43), calls=%async_computation | async-start | bytes 7340032 | tf_op jit(solution)/shard_map/all_to_all | solution.py:50
  38.9 0.6 dynamic_slice.3
  40.1 121.6 %all-to-all-done = bf16[16,32,3584]{2,1,0:T(8,128)(2,1)} async-done(((bf16[16,32,3584]{2,1,0:T(8,128)(2,1)}), bf16[16,32,3584]{2,1,0:T(8,128)(2,1)}, u32[]{:S(2)}, u32[]{:S(2)}) %all-to-all-start) | async-done | bytes 3670048 | tf_op jit(solution)/shard_map/all_to_all | solution.py:50
  161.8 528.8 %all-reduce.3.cloned.1.call-done = (bf16[2,3584,1024]{2,1,0:T(8,128)(2,1)}, bf16[1024,3584]{1,0:T(8,128)(2,1)}) async-done(((bf16[2,3584,1024]{2,1,0:T(8,128)(2,1)}, bf16[1024,3584]{1,0:T(8,128)(2,1)}), (bf16[2,3584,1024]{2,1,0:T(8,128)(2,1)}, bf16[1024,3584]{1,0:T(8,128)(2,1)})) %all-reduce.3.cloned.1.call-update) | async-done | bytes 22020112 | tf_op jit(solution)/shard_map/psum | solution.py:9
  690.6 7.5 fusion.4
  698.1 2.1 copy-done.5
  700.2 6.0 fusion.1
  706.2 2.5 pad_maximum_fusion
  708.8 13.0 %reduce-scatter.2.cloned.1.call-done = f32[512,1024]{0,1:T(8,128)} async-done(((f32[1024,1024]{0,1:T(8,128)}), f32[512,1024]{0,1:T(8,128)}) %reduce-scatter.2.cloned.1.call-update) | async-done | bytes 2097168 | tf_op jit(solution)/shard_map/reduce_scatter | solution.py:17
  721.8 2.7 fusion.11
  724.5 10.5 %all-gather.2.cloned.1.call-done = bf16[1024,512]{0,1:T(8,128)(2,1)} async-done(((bf16[512,512]{0,1:T(8,128)(2,1)}), bf16[1024,512]{0,1:T(8,128)(2,1)}) %all-gather.2.cloned.1.call-update) | async-done | bytes 1048592 | tf_op jit(solution)/shard_map/all_gather | solution.py:23
  735.0 9.5 %fusion.10 = bf16[512,3584]{1,0:T(8,128)(2,1)S(1)} fusion(bf16[1024,512]{0,1:T(8,128)(2,1)} %all-gather.2.cloned.1.call-done, bf16[1024,3584]{1,0:T(8,128)(2,1)} %get-tuple-element.8, bf16[1,1024,3584]{2,1,0:T(8,128)(2,1)} %param.10, pred[]{:T(512)S(6)} %ne.6), kind=kOutput, calls=%fused_computation.13 | convolution fusion | flops 3763601408 | bytes 19398656 | tf_op jit(solution)/shard_map/dot_general | solution.py:22
  744.5 88.6 %all_to_all.24 = bf16[16,32,3584]{2,1,0:T(8,128)(2,1)S(1)} all-to-all(bf16[16,32,3584]{2,1,0:T(8,128)(2,1)S(1)} %bitcast.47), channel_id=1, replica_groups=mesh['ep'=2,'dp'=16] {'dp'}, dimensions={0} | all-to-all | bytes 7340032 | tf_op jit(solution)/shard_map/all_to_all | solution.py:65
  833.1 2.6 convolution_convert_fusion.1
  (31 shorter events, 0.6 us)
Async XLA Ops:
  6.5 20.7 %copy-start = (bf16[32,3584]{1,0:T(8,128)(2,1)S(1)}, bf16[32,3584]{1,0:T(8,128)(2,1)}, u32[]{:S(2)}) copy-start(bf16[32,3584]{1,0:T(8,128)(2,1)} %param.7) | copy-start | bytes 688132
  6.5 684.0 %all-reduce.3.cloned.1.call-start = ((), (), s32[]{:S(2)}) async-start(), calls=%async_computation.5 | async-start | bytes 44040192 | tf_op jit(solution)/shard_map/psum | solution.py:9
  8.5 6.7 copy-start.2
  24.8 0.7 copy-start.3
  24.8 2.0 copy-start.4
  25.4 13.4 %copy-start.6 = (s32[16]{0:T(128)S(1)}, s32[16]{0:T(128)}, u32[]{:S(2)}) copy-start(s32[16]{0:T(128)} %param.13) | copy-start | bytes 196
  30.2 667.9 %slice-start = ((s8[7340032]{0:T(1024)(128)(4,1)}), s8[3145728]{0:T(1024)(128)(4,1)S(1)}, s32[]{:S(2)}) async-start(s8[7340032]{0:T(1024)(128)(4,1)} %bitcast.45), calls=%async_computation.6 | async-start | bytes 6291456
  30.2 131.6 %all-to-all-start = ((bf16[16,32,3584]{2,1,0:T(8,128)(2,1)}), bf16[16,32,3584]{2,1,0:T(8,128)(2,1)}, u32[]{:S(2)}, u32[]{:S(2)}) async-start(bf16[16,32,3584]{2,1,0:T(8,128)(2,1)} %bitcast.43), calls=%async_computation | async-start | bytes 7340032 | tf_op jit(solution)/shard_map/all_to_all | solution.py:50
  38.8 683.0 %reduce-scatter.2.cloned.1.call-start = ((), (), s32[]{:S(2)}) async-start(), calls=%async_computation.3 | async-start | bytes 6291456 | tf_op jit(solution)/shard_map/reduce_scatter | solution.py:17
  690.6 7.5 slice-start.1
  690.6 9.6 %copy-start.5 = (bf16[2,3584,1024]{2,1,0:T(8,128)(2,1)S(1)}, bf16[2,3584,1024]{2,1,0:T(8,128)(2,1)}, u32[]{:S(2)}) copy-start(bf16[2,3584,1024]{2,1,0:T(8,128)(2,1)} %get-tuple-element.7) | copy-start | bytes 44040196
  708.7 26.2 %all-gather.2.cloned.1.call-start = ((), (), s32[]{:S(2)}) async-start(), calls=%async_computation.4 | async-start | bytes 1572864 | tf_op jit(solution)/shard_map/all_gather | solution.py:23
  735.0 100.7 %copy-start.1 = (bf16[32,3584]{1,0:T(8,128)(2,1)S(1)}, bf16[32,3584]{1,0:T(8,128)(2,1)}, u32[]{:S(2)}) copy-start(bf16[32,3584]{1,0:T(8,128)(2,1)} %param.7) | copy-start | bytes 688132
Sparse Core Ops, SparseCore 0:
  24.9 665.6 all-reduce.2
  708.9 12.9 reduce-scatter.1
  724.6 10.3 all-gather.1
where the time goes:
time: 843 us; the launch traced here: 842 us
  waiting for transfers between devices  674 us (80%)
  blocking collectives  88.6 us (11%)
  matrix products  28.5 us (3%)
  other arithmetic  23.9 us (3%)
  between operations  14.5 us (2%)
  starting transfers between devices  8.74 us (1%)
    psum x1, waiting for transfers between devices, spread(): return lax.psum(kept, axis)  529 us
    all_to_all x1, waiting for transfers between devices, per_device(): lax.all_to_all(outgoing, 'dp', split_axis=0, concat_axis=0, tiled=True)  122 us
    all_to_all x1, blocking collectives, per_device(): lax.all_to_all(results, 'dp', split_axis=0, concat_axis=0, tiled=True)  88.6 us
  transfers between devices with their start and end apart: 4, of which 4 were waited for; matrix products, arithmetic and copies ran while one was open for 1% of the time, Pallas kernels for 0%

commit v1 on v0

v1 whole, which is shorter than its diff:
```python
import jax
import jax.numpy as jnp
from jax import lax
from jax.sharding import PartitionSpec as P


def per_device(tokens, gate_weight, up_weight, down_weight, targets, mixing, move_plan):
    groups = lax.axis_size("dp")
    me = lax.axis_index("dp")
    lanes = jnp.arange(groups, dtype=jnp.int32)
    anchors = jnp.sum(
        jnp.where(targets[:, :, None] == lanes, move_plan[None, None, :], 0), axis=2
    )
    share = jnp.sum(
        jnp.where(anchors[:, :, None] == lanes, mixing[:, :, None], 0.0), axis=1
    )
    shares = lax.all_gather(share, "dp", axis=0, tiled=True)
    rows = lax.all_gather(tokens, "dp", axis=0, tiled=True)
    width = rows.shape[0]
    dims = (((0,), (1,)), ((), ()))
    gate_term = lax.dot_general(gate_weight[0], rows, dims, preferred_element_type=jnp.float32)
    up_term = lax.dot_general(up_weight[0], rows, dims, preferred_element_type=jnp.float32)
    summed = lax.psum_scatter(
        jnp.concatenate([gate_term, up_term], axis=1), "ep", scatter_dimension=0, tiled=True
    )
    hidden = (jax.nn.silu(summed[:, :width]) * summed[:, width:]).astype(jnp.bfloat16)
    output = lax.dot_general(
        lax.all_gather(hidden, "ep", axis=0, tiled=True),
        down_weight[0],
        (((0,), (0,)), ((), ())),
        preferred_element_type=jnp.float32,
    )
    scale = jnp.sum(jnp.where(lanes == me, shares, 0.0), axis=1, keepdims=True)
    scaled = output.astype(jnp.bfloat16).astype(jnp.float32) * scale
    mixed = lax.psum_scatter(scaled.astype(jnp.bfloat16), "dp", scatter_dimension=0, tiled=True)
    return mixed.astype(jnp.bfloat16)


def solution(mesh):
    return jax.shard_map(
        per_device,
        mesh=mesh,
        in_specs=(
            P("dp", "ep"),
            P("dp", "ep", None),
            P("dp", "ep", None),
            P("dp", None, "ep"),
            P("dp", None),
            P("dp", None),
            P(),
        ),
        out_specs=P("dp", "ep"),
        check_vma=False,
    )
```

time: 843 us -> 255 us (0.30)
  waiting for transfers between devices: 674 us -> 170 us
  blocking collectives: 88.6 us -> 41.6 us
  other arithmetic: 23.9 us -> 5.28 us
  starting transfers between devices: 8.74 us -> 0.12 us
    psum x1 -> x0, waiting for transfers between devices: 529 us -> none  [spread(): return lax.psum(kept, axis)]
    all_to_all x1 -> x0, waiting for transfers between devices: 122 us -> none  [per_device(): lax.all_to_all(outgoing, 'dp', split_axis=0, concat_axis=0, tiled=True)]
    all_to_all x1 -> x0, blocking collectives: 88.6 us -> none  [per_device(): lax.all_to_all(results, 'dp', split_axis=0, concat_axis=0, tiled=True)]
    reduce_scatter x1 -> x2, waiting for transfers between devices: 13 us -> 92.3 us  [the longest x1 81.7 us: per_device(): lax.psum_scatter(scaled.astype(jnp.bfloat16), 'dp', scatter_dimension=0,...]
    all_gather x1 -> x2, waiting for transfers between devices: 10.5 us -> 77.2 us  [the longest x1 77.2 us: per_device(): rows = lax.all_gather(tokens, 'dp', axis=0, tiled=True)]
    all_gather x0 -> x1, blocking collectives: none -> 41.6 us  [per_device(): shares = lax.all_gather(share, 'dp', axis=0, tiled=True)]
    select_n x2 -> x0, other arithmetic: 16.2 us -> none  [spread(): jnp.where(lax.axis_index(axis) == source, value, 0).astype(value.dtype)]
    all_to_all x1 -> x0, starting transfers between devices: 8.66 us -> none  [per_device(): lax.all_to_all(outgoing, 'dp', split_axis=0, concat_axis=0, tiled=True)]
  transfers between devices with their start and end apart: 4 -> 4, of which waited for: 4 -> 3; matrix products, arithmetic and copies ran while one was open for 1% -> 0% of each run, Pallas kernels for 0% -> 0%
where the time goes in v1:
time: 255 us; the launch traced here: 254 us
  waiting for transfers between devices  170 us (67%)
  blocking collectives  41.6 us (16%)
  matrix products  23.7 us (9%)
  between operations  13.2 us (5%)
  other arithmetic  5.28 us (2%)
    reduce_scatter x1, waiting for transfers between devices, per_device(): lax.psum_scatter(scaled.astype(jnp.bfloat16), 'dp', scatter_dimension=0,...  81.7 us
    all_gather x1, waiting for transfers between devices, per_device(): rows = lax.all_gather(tokens, 'dp', axis=0, tiled=True)  77.2 us
    all_gather x1, blocking collectives, per_device(): shares = lax.all_gather(share, 'dp', axis=0, tiled=True)  41.6 us
    reduce_scatter x1, waiting for transfers between devices, per_device(): lax.psum_scatter(jnp.concatenate([gate_term, up_term], axis=1), 'ep', sca...  10.5 us
    dot_general x1, matrix products, per_device(): lax.dot_general(lax.all_gather(hidden, 'ep', axis=0, tiled=True), down_we...  9.17 us
    dot_general x1, matrix products, per_device(): lax.dot_general(up_weight[0], rows, dims, preferred_element_type=jnp.floa...  8.2 us
    dot_general x1, matrix products, per_device(): lax.dot_general(gate_weight[0], rows, dims, preferred_element_type=jnp.fl...  6.37 us
  transfers between devices with their start and end apart: 4, of which 3 were waited for; matrix products, arithmetic and copies ran while one was open for 0% of the time, Pallas kernels for 0%

profile of v1, /device:TPU:0, one launch (start us, length us, event | category | flops | bytes accessed | tf_op | source)
XLA Modules:
  0.0 254.3 jit_solution(12130641132115662548)
XLA Ops:
  6.5 0.0 all-gather.4.cloned.1.call-start
  6.5 0.7 all-gather.4.cloned.1.call-update
  7.3 0.0 reduce-scatter.3.cloned.1.call-start
  7.3 77.2 %all-gather.4.cloned.1.call-done = bf16[512,3584]{1,0:T(8,128)(2,1)} async-done(((bf16[32,3584]{1,0:T(8,128)(2,1)}), bf16[512,3584]{1,0:T(8,128)(2,1)}) %all-gather.4.cloned.1.call-update) | async-done | bytes 3670032 | tf_op jit(solution)/shard_map/all_gather | solution.py:18
  84.5 8.2 %fusion.2 = f32[1024,512]{0,1:T(8,128)S(1)} fusion(bf16[512,3584]{1,0:T(8,128)(2,1)} %all-gather.4.cloned.1.call-done, bf16[1,3584,1024]{2,1,0:T(8,128)(2,1)} %param.9), kind=kOutput, calls=%fused_computation.2 | convolution fusion | flops 3758096384 | bytes 13107200 | tf_op jit(solution)/shard_map/dot_general | solution.py:22
  92.7 0.0 copy-done.3
  92.7 6.4 %fusion.4 = f32[1024,512]{0,1:T(8,128)S(1)} fusion(bf16[512,3584]{1,0:T(8,128)(2,1)S(1)} %copy-done.3, bf16[1,3584,1024]{2,1,0:T(8,128)(2,1)} %param.8), kind=kOutput, calls=%fused_computation.4 | convolution fusion | flops 3758096384 | bytes 13107200 | tf_op jit(solution)/shard_map/dot_general | solution.py:21
  99.1 2.5 pad_maximum_fusion
  101.5 0.0 reduce-scatter.3.cloned.1.call-update
  101.6 0.0 all-gather.6.cloned.1.call-start
  101.6 10.5 %reduce-scatter.3.cloned.1.call-done = f32[512,1024]{0,1:T(8,128)} async-done(((f32[1024,1024]{0,1:T(8,128)}), f32[512,1024]{0,1:T(8,128)}) %reduce-scatter.3.cloned.1.call-update) | async-done | bytes 2097168 | tf_op jit(solution)/shard_map/reduce_scatter | solution.py:23
  112.1 2.6 %fusion.11 = bf16[512,512]{0,1:T(8,128)(2,1)} fusion(f32[512,1024]{0,1:T(8,128)} %reduce-scatter.3.cloned.1.call-done), kind=kLoop, calls=%fused_computation.10 | loop fusion | flops 1572864 | bytes 2621440 | tf_op jit(solution)/shard_map/convert_element_type | solution.py:26
  114.8 0.0 all-gather.6.cloned.1.call-update
  114.8 0.0 reduce-scatter.5.cloned.1.call-start
  114.8 0.0 copy-done
  114.8 0.0 copy-done.2
  114.8 0.1 select_reduce_fusion.1
  115.0 41.6 %all-gather = f32[16,32,16]{1,2,0:T(8,128)S(1)} all-gather(f32[1,32,16]{1,2,0:T(8,128)S(1)} %bitcast.19), channel_id=1, replica_groups=mesh['ep'=2,'dp'=16] {'dp'}, dimensions={0}, use_global_device_ids=true | all-gather | bytes 34816 | tf_op jit(solution)/shard_map/all_gather | solution.py:17
  156.7 0.1 reshape.6
  156.8 0.1 select_reduce_fusion.2
  156.9 0.0 all-gather.6.cloned.1.call-done
  156.9 9.2 %multiply_convert_fusion = bf16[512,3584]{1,0:T(8,128)(2,1)} fusion(bf16[1024,512]{0,1:T(8,128)(2,1)} %all-gather.6.cloned.1.call-done, bf16[1,1024,3584]{2,1,0:T(8,128)(2,1)} %param.10, f32[512]{0:T(512)S(1)} %select_reduce_fusion.2), kind=kOutput, calls=%fused_computation.6 | convolution fusion | flops 3765436416 | bytes 12060672 | tf_op jit(solution)/shard_map/dot_general | solution.py:27
  166.1 0.0 reduce-scatter.5.cloned.1.call-update
  166.1 81.7 %reduce-scatter.5.cloned.1.call-done = bf16[32,3584]{1,0:T(8,128)(2,1)} async-done(((bf16[512,3584]{1,0:T(8,128)(2,1)}), bf16[32,3584]{1,0:T(8,128)(2,1)}) %reduce-scatter.5.cloned.1.call-update) | async-done | bytes 229392 | tf_op jit(solution)/shard_map/reduce_scatter | solution.py:35
  (8 shorter events, 0.1 us)
Async XLA Ops:
  6.5 77.9 %all-gather.4.cloned.1.call-start = ((), (), s32[]{:S(2)}) async-start(), calls=%async_computation.2 | async-start | bytes 3899392 | tf_op jit(solution)/shard_map/all_gather | solution.py:18
  7.3 104.9 %reduce-scatter.3.cloned.1.call-start = ((), (), s32[]{:S(2)}) async-start(), calls=%async_computation.3 | async-start | bytes 6291456 | tf_op jit(solution)/shard_map/reduce_scatter | solution.py:23
  84.5 8.2 %copy-start.3 = (bf16[512,3584]{1,0:T(8,128)(2,1)S(1)}, bf16[512,3584]{1,0:T(8,128)(2,1)}, u32[]{:S(2)}) copy-start(bf16[512,3584]{1,0:T(8,128)(2,1)} %all-gather.4.cloned.1.call-done) | copy-start | bytes 11010052
  101.5 13.3 %copy-start = (s32[32,8]{0,1:T(8,128)S(1)}, s32[32,8]{0,1:T(8,128)}, u32[]{:S(2)}) copy-start(s32[32,8]{0,1:T(8,128)} %param.11) | copy-start | bytes 3076
  101.5 13.3 %copy-start.2 = (s32[16]{0:T(128)S(1)}, s32[16]{0:T(128)}, u32[]{:S(2)}) copy-start(s32[16]{0:T(128)} %param.13) | copy-start | bytes 196
  101.5 13.4 %copy-start.1 = (f32[32,8]{0,1:T(8,128)S(1)}, f32[32,8]{0,1:T(8,128)}, u32[]{:S(2)}) copy-start(f32[32,8]{0,1:T(8,128)} %param.12) | copy-start | bytes 3076
  101.6 55.3 %all-gather.6.cloned.1.call-start = ((), (), s32[]{:S(2)}) async-start(), calls=%async_computation.4 | async-start | bytes 1572864 | tf_op jit(solution)/shard_map/all_gather | solution.py:28
  114.8 133.0 %reduce-scatter.5.cloned.1.call-start = ((), (), s32[]{:S(2)}) async-start(), calls=%async_computation.5 | async-start | bytes 3899392 | tf_op jit(solution)/shard_map/reduce_scatter | solution.py:35
Sparse Core Ops, SparseCore 0:
  10.1 74.3 all-gather.3
  101.7 10.4 reduce-scatter.2
  114.9 10.2 all-gather.5
  166.2 81.5 reduce-scatter.4

commit v2 on v1

v2 whole, which is shorter than its diff:
```python
import functools

import jax
import jax.numpy as jnp
from jax import lax
from jax.experimental import pallas as pl
from jax.experimental.pallas import tpu as pltpu
from jax.sharding import PartitionSpec as P

MESH = pl.DeviceIdType.MESH
F32, BF16 = jnp.float32, jnp.bfloat16
PLANE, LINE = 4, 4


def share_of(targets, mixing, move_plan, lanes):
    anchors = jnp.sum(
        jnp.where(targets[:, :, None] == lanes, move_plan[None, None, :], 0), axis=2
    )
    return jnp.sum(jnp.where(anchors[:, :, None] == lanes, mixing[:, :, None], 0.0), axis=1)


def tile_of(extent, largest):
    return next(t for t in (512, 256, 128) if t <= largest and extent % t == 0)


def kernel(
    groups, ext, gate_hbm, up_hbm, down_hbm, out,
    gate, up, down, tok, psend, precv, pown, hid, cont, dsend, dland,
    xsend, ysend, xland, yland, zsend, zland, acc,
    wsem, own_sem, col_s, col_r, ag_s, ag_r, ep_s, ep_r, rs_s, rs_r, z_s, z_r,
):
    me = lax.axis_index("dp")
    core = lax.axis_index("ep")
    rows = ext.shape[0]
    half = rows // 2
    wide = gate.shape[0]
    keep = psend.shape[2] // 2
    block = PLANE * rows
    z = me // PLANE
    j = me % PLANE
    y, x = j // 2, j % 2
    jx, jy, jd = y * 2 + 1 - x, (1 - y) * 2 + x, (1 - y) * 2 + 1 - x
    dx, dy = z * PLANE + jx, z * PLANE + jy
    top = z // 2
    inner = z + top * (LINE - 1 - 2 * z)
    mirrored = (inner, 1 - inner, 2, 3)
    plane = [q + top * (LINE - 1 - 2 * q) for q in mirrored]

    weight_copies = [
        pltpu.make_async_copy(gate_hbm, gate, wsem.at[0]),
        pltpu.make_async_copy(up_hbm, up, wsem.at[1]),
        pltpu.make_async_copy(down_hbm, down, wsem.at[2]),
    ]
    for c in weight_copies:
        c.start()

    def at_rows(slot):
        return pl.ds(pl.multiple_of(slot * rows, rows), rows)

    def at_half(slot, h):
        return pl.ds(pl.multiple_of(slot * rows + h * half, half), half)

    own_copy = pltpu.make_async_copy(ext, tok.at[at_rows(me)], own_sem.at[0])
    own_copy.start()

    peers = [plane[i] * PLANE + j for i in range(1, LINE)]
    barrier = pltpu.get_barrier_semaphore()
    for d in [dx, dy] + peers:
        pl.semaphore_signal(barrier, inc=1, device_id={"dp": d}, device_id_type=MESH)
    pl.semaphore_signal(barrier, inc=1, device_id={"ep": 1 - core}, device_id_type=MESH)
    pl.semaphore_wait(barrier, len(peers) + 3)

    started = []

    def send(src, dst, ss, rs, device):
        c = pltpu.make_async_remote_copy(
            src_ref=src, dst_ref=dst, send_sem=ss, recv_sem=rs,
            device_id=device, device_id_type=MESH,
        )
        c.start()
        started.append(c)

    def landed(dst, ss, rs, device):
        pltpu.make_async_remote_copy(
            src_ref=dst, dst_ref=dst, send_sem=ss, recv_sem=rs,
            device_id=device, device_id_type=MESH,
        ).wait_recv()

    X, Y, E = {"dp": dx}, {"dp": dy}, {"ep": 1 - core}

    def spread_xy(s):
        src = ext if s == 0 else tok.at[at_rows(plane[s] * PLANE + j)]
        dst = tok.at[at_rows(plane[s] * PLANE + j)]
        send(src, dst, ag_s.at[0, s], ag_r.at[0, s], X)
        send(src, dst, ag_s.at[1, s], ag_r.at[1, s], Y)

    def column_forward(s):
        landed(tok.at[at_rows(plane[s] * PLANE + j)], col_s.at[s - 1], col_r.at[plane[s]], X)
        spread_xy(s)

    def half_forward(s):
        base = plane[s] * PLANE
        landed(tok.at[at_rows(base + jx)], ag_s.at[0, s], ag_r.at[0, s], X)
        part = tok.at[at_half(base + jx, 0)]
        send(part, part, ag_s.at[2, s], ag_r.at[2, s], Y)
        landed(tok.at[at_rows(base + jy)], ag_s.at[1, s], ag_r.at[1, s], Y)
        part = tok.at[at_half(base + jy, 1)]
        send(part, part, ag_s.at[3, s], ag_r.at[3, s], X)

    def diag_wait(s):
        base = plane[s] * PLANE
        landed(tok.at[at_half(base + jd, 0)], ag_s.at[2, s], ag_r.at[2, s], Y)
        landed(tok.at[at_half(base + jd, 1)], ag_s.at[3, s], ag_r.at[3, s], X)

    gtile = tile_of(keep, 256)

    def project(s, side, put):
        here = pl.ds(pl.multiple_of(plane[s] * block, block), block)

        @pl.loop(0, keep // gtile)
        def _(n):
            off = pl.multiple_of(n * gtile, gtile)
            src = pl.ds(pl.multiple_of(side * keep + off, gtile), gtile)
            lhs = tok[here, pl.ds(0, wide)]
            put[:, pl.ds(off, gtile)] = jnp.dot(lhs, gate[:, src], preferred_element_type=F32)
            put[:, pl.ds(pl.multiple_of(keep + off, gtile), gtile)] = jnp.dot(
                lhs, up[:, src], preferred_element_type=F32
            )

    def hide(s):
        landed(precv.at[s], ep_s.at[0, s], ep_r.at[0, s], E)
        g = pown[:, pl.ds(0, keep)] + precv[s, :, pl.ds(0, keep)]
        u = pown[:, pl.ds(keep, keep)] + precv[s, :, pl.ds(keep, keep)]
        hid[s, core] = (g / (1.0 + jnp.exp(-g)) * u).astype(BF16)
        send(hid.at[s, core], hid.at[s, core], ep_s.at[1, s], ep_r.at[1, s], E)

    dtile = tile_of(wide, 512)

    def lower(s):
        here = pl.ds(pl.multiple_of(plane[s] * block, block), block)
        packed = tok[here, pl.ds(wide, tok.shape[1] - wide)].astype(F32)
        lane = lax.broadcasted_iota(jnp.int32, packed.shape, 1)
        share = jnp.sum(jnp.where(lane % groups == me, packed, 0.0), axis=1, keepdims=True)
        landed(hid.at[s, 1 - core], ep_s.at[1, s], ep_r.at[1, s], E)

        @pl.loop(0, wide // dtile)
        def _(n):
            cols = pl.ds(pl.multiple_of(n * dtile, dtile), dtile)
            e = jnp.dot(hid[s, 0], down[pl.ds(0, keep), cols], preferred_element_type=F32)
            e += jnp.dot(hid[s, 1], down[pl.ds(keep, keep), cols], preferred_element_type=F32)
            cont[s, :, cols] = e.astype(BF16).astype(F32) * share

        dsend[s] = cont[s, at_rows(jd)].astype(BF16)
        send(dsend.at[s, pl.ds(0, half)], dland.at[s, pl.ds(0, half)], rs_s.at[0, s], rs_r.at[0, s], Y)
        send(dsend.at[s, pl.ds(half, half)], dland.at[s, pl.ds(half, half)], rs_s.at[1, s], rs_r.at[1, s], X)

    def reduce_first(s):
        landed(dland.at[s, pl.ds(0, half)], rs_s.at[0, s], rs_r.at[0, s], Y)
        xsend[s, pl.ds(0, half)] = (
            cont[s, at_half(jx, 0)] + dland[s, pl.ds(0, half)].astype(F32)
        ).astype(BF16)
        xsend[s, pl.ds(half, half)] = cont[s, at_half(jx, 1)].astype(BF16)
        send(xsend.at[s], xland.at[s], rs_s.at[2, s], rs_r.at[2, s], X)
        landed(dland.at[s, pl.ds(half, half)], rs_s.at[1, s], rs_r.at[1, s], X)
        ysend[s, pl.ds(0, half)] = cont[s, at_half(jy, 0)].astype(BF16)
        ysend[s, pl.ds(half, half)] = (
            cont[s, at_half(jy, 1)] + dland[s, pl.ds(half, half)].astype(F32)
        ).astype(BF16)
        send(ysend.at[s], yland.at[s], rs_s.at[3, s], rs_r.at[3, s], Y)

    def reduce_second(s):
        landed(xland.at[s], rs_s.at[2, s], rs_r.at[2, s], X)
        landed(yland.at[s], rs_s.at[3, s], rs_r.at[3, s], Y)
        total = cont[s, at_rows(j)] + xland[s].astype(F32) + yland[s].astype(F32)
        if s == 0:
            acc[...] = total
        else:
            zsend[s] = total.astype(BF16)
            send(zsend.at[s], zland.at[z], z_s.at[s], z_r.at[z], {"dp": peers[s - 1]})

    spread_xy(0)
    for i in range(1, LINE):
        send(ext, tok.at[at_rows(me)], col_s.at[i - 1], col_r.at[z], {"dp": peers[i - 1]})
    half_forward(0)
    column_forward(1)
    own_copy.wait()
    for s in range(LINE):
        diag_wait(s)
        if s == 0:
            weight_copies[0].wait()
            weight_copies[1].wait()
        project(s, 1 - core, psend.at[s])
        send(psend.at[s], precv.at[s], ep_s.at[0, s], ep_r.at[0, s], E)
        project(s, core, pown)
        hide(s)
        if s + 1 < LINE:
            half_forward(s + 1)
        if s + 2 < LINE:
            column_forward(s + 2)
        if s >= 1:
            reduce_first(s - 1)
        if s >= 2:
            reduce_second(s - 2)
        if s == 0:
            weight_copies[2].wait()
        lower(s)
    reduce_first(LINE - 1)
    reduce_second(LINE - 2)
    reduce_second(LINE - 1)
    total = acc[...]
    for s in range(1, LINE):
        landed(zland.at[plane[s]], z_s.at[s], z_r.at[plane[s]], X)
        total += zland[plane[s]].astype(F32)
    out[...] = total.astype(BF16)
    for c in started:
        c.wait_send()


def fused(tokens, gate_weight, up_weight, down_weight, targets, mixing, move_plan):
    groups = lax.axis_size("dp")
    rows, wide = tokens.shape
    lanes = jnp.arange(groups, dtype=jnp.int32)
    share = share_of(targets, mixing, move_plan, lanes)
    high = lax.reduce_precision(share, 8, 7)
    middle = lax.reduce_precision(share - high, 8, 7)
    low = share - high - middle
    pad = -(3 * groups) % 128
    ext = jnp.concatenate(
        [tokens, high.astype(BF16), middle.astype(BF16), low.astype(BF16), jnp.zeros((rows, pad), BF16)],
        axis=1,
    )
    full = gate_weight.shape[2]
    keep = full // lax.axis_size("ep")
    block = PLANE * rows
    VM, DMA = pltpu.VMEM, pltpu.SemaphoreType.DMA
    return pl.pallas_call(
        functools.partial(kernel, groups),
        out_shape=jax.ShapeDtypeStruct((rows, wide), BF16),
        in_specs=[pl.BlockSpec(memory_space=pltpu.VMEM)] + [pl.BlockSpec(memory_space=pl.ANY)] * 3,
        out_specs=pl.BlockSpec(memory_space=pltpu.VMEM),
        scratch_shapes=[
            VM((wide, full), BF16), VM((wide, full), BF16), VM((full, wide), BF16),
            VM((groups * rows, ext.shape[1]), BF16),
            VM((LINE, block, 2 * keep), F32), VM((LINE, block, 2 * keep), F32),
            VM((block, 2 * keep), F32), VM((LINE, 2, block, keep), BF16),
            VM((LINE, block, wide), F32),
            VM((LINE, rows, wide), BF16), VM((LINE, rows, wide), BF16),
            VM((LINE, rows, wide), BF16), VM((LINE, rows, wide), BF16),
            VM((LINE, rows, wide), BF16), VM((LINE, rows, wide), BF16),
            VM((LINE, rows, wide), BF16), VM((LINE, rows, wide), BF16),
            VM((rows, wide), F32),
            DMA((3,)), DMA((1,)), DMA((LINE - 1,)), DMA((LINE,)),
            DMA((4, LINE)), DMA((4, LINE)), DMA((2, LINE)), DMA((2, LINE)),
            DMA((4, LINE)), DMA((4, LINE)), DMA((LINE,)), DMA((LINE,)),
        ],
        compiler_params=pltpu.CompilerParams(
            collective_id=0, has_side_effects=True, vmem_limit_bytes=63 * 1024 * 1024
        ),
    )(ext, gate_weight[0], up_weight[0], down_weight[0])


def plain(tokens, gate_weight, up_weight, down_weight, targets, mixing, move_plan):
    groups = lax.axis_size("dp")
    me = lax.axis_index("dp")
    lanes = jnp.arange(groups, dtype=jnp.int32)
    share = share_of(targets, mixing, move_plan, lanes)
    shares = lax.all_gather(share, "dp", axis=0, tiled=True)
    rows = lax.all_gather(tokens, "dp", axis=0, tiled=True)
    width = rows.shape[0]
    dims = (((0,), (1,)), ((), ()))
    gate_term = lax.dot_general(gate_weight[0], rows, dims, preferred_element_type=F32)
    up_term = lax.dot_general(up_weight[0], rows, dims, preferred_element_type=F32)
    summed = lax.psum_scatter(
        jnp.concatenate([gate_term, up_term], axis=1), "ep", scatter_dimension=0, tiled=True
    )
    hidden = (jax.nn.silu(summed[:, :width]) * summed[:, width:]).astype(BF16)
    output = lax.dot_general(
        lax.all_gather(hidden, "ep", axis=0, tiled=True),
        down_weight[0],
        (((0,), (0,)), ((), ())),
        preferred_element_type=F32,
    )
    scale = jnp.sum(jnp.where(lanes == me, shares, 0.0), axis=1, keepdims=True)
    scaled = output.astype(BF16).astype(F32) * scale
    return lax.psum_scatter(scaled.astype(BF16), "dp", scatter_dimension=0, tiled=True)


def solution(mesh):
    small = mesh.shape["dp"] == PLANE * LINE and mesh.shape["ep"] == 2
    return jax.shard_map(
        fused if small else plain,
        mesh=mesh,
        in_specs=(
            P("dp", "ep"),
            P("dp", "ep", None),
            P("dp", "ep", None),
            P("dp", None, "ep"),
            P("dp", None),
            P("dp", None),
            P(),
        ),
        out_specs=P("dp", "ep"),
        check_vma=False,
    )
```

time: 255 us -> 95.5 us (0.37)
  waiting for transfers between devices: 170 us -> 0 us
  Pallas kernels: 0 us -> 90.2 us
  blocking collectives: 41.6 us -> 0 us
  matrix products: 23.7 us -> 0 us
  between operations: 13.2 us -> 0.03 us
  other arithmetic: 5.28 us -> 1.51 us
  local copies, waits for them, and re-layouts: 0.16 us -> 3.5 us
    reduce_scatter x2 -> x0, waiting for transfers between devices: 92.3 us -> none  [the longest x1 81.7 us: per_device(): lax.psum_scatter(scaled.astype(jnp.bfloat16), 'dp', scatter_dimension=0,...]
    pallas_call x0 -> x1, Pallas kernels: none -> 90.2 us  [fused(): pl.pallas_call(functools.partial(kernel, groups), out_shape=jax.ShapeDtyp...]
    all_gather x2 -> x0, waiting for transfers between devices: 77.2 us -> none  [the longest x1 77.2 us: per_device(): rows = lax.all_gather(tokens, 'dp', axis=0, tiled=True)]
    all_gather x1 -> x0, blocking collectives: 41.6 us -> none  [per_device(): shares = lax.all_gather(share, 'dp', axis=0, tiled=True)]
    dot_general x3 -> x0, matrix products: 23.7 us -> none  [the longest x1 9.17 us: per_device(): lax.dot_general(lax.all_gather(hidden, 'ep', axis=0, tiled=True), down_we...]
    convert_element_type x1, other arithmetic: 2.62 us -> 0.01 us  [fused(): low.astype(BF16)]
  transfers between devices with their start and end apart: 4 -> 0, of which waited for: 3 -> 0; matrix products, arithmetic and copies ran while one was open for 0% -> 0% of each run, Pallas kernels for 0% -> 0%
where the time goes in v2:
time: 95.5 us; the launch traced here: 95.3 us
  Pallas kernels  90.2 us (94%)
  local copies, waits for them, and re-layouts  3.5 us (4%)
  other arithmetic  1.51 us (2%)
    pallas_call x1, Pallas kernels, fused(): pl.pallas_call(functools.partial(kernel, groups), out_shape=jax.ShapeDtyp...  90.2 us

profile of v2, /device:TPU:0, one launch (start us, length us, event | category | flops | bytes accessed | tf_op | source)
XLA Modules:
  0.0 95.3 jit_solution(8750795272916267235)
XLA Ops:
  0.0 0.8 select_reduce_fusion.1
  0.8 0.7 select_reduce_fusion
  1.5 0.1 copy.13
  1.6 0.1 copy.12
  1.7 1.7 %concatenate.3.ext = bf16[32,3712]{1,0:T(8,128)(2,1)} concatenate(bf16[32,3584]{1,0:T(8,128)(2,1)} %param.7, bf16[32,16]{1,0:T(8,128)(2,1)S(1)} %get-tuple-element.7, bf16[32,16]{1,0:T(8,128)(2,1)S(1)} %get-tuple-element.6, bf16[32,16]{1,0:T(8,128)(2,1)S(1)} %get-tuple-element.5, bf16[32,80]{1,0:T(8,128)(2,1)S(1)} %broadcast_in_dim.37), dimensions={1} | concatenate | bytes 475136 | tf_op jit(solution)/shard_map/concatenate | solution.py:228
  3.4 90.2 %shard_map.73 = bf16[32,3584]{1,0:T(8,128)(2,1)} custom-call(bf16[32,3712]{1,0:T(8,128)(2,1)} %concatenate.3.ext, bf16[3584,1024]{1,0:T(8,128)(2,1)} %bitcast.3, bf16[3584,1024]{1,0:T(8,128)(2,1)} %bitcast.4, bf16[1024,3584]{1,0:T(8,128)(2,1)} %bitcast.5), custom_call_target="tpu_custom_call" | custom-call | tf_op jit(solution)/shard_map/pallas_call | solution.py:236
  93.6 1.6 %copy.16 = bf16[32,3584]{1,0:T(8,128)(2,1)} copy(bf16[32,3584]{1,0:T(8,128)(2,1)} %shard_map.73) | data formatting | bytes 458752
  (3 shorter events, 0.0 us)

commit v3 on v2

--- a/solution.py
+++ b/solution.py
@@ -51,9 +51,6 @@
         pltpu.make_async_copy(up_hbm, up, wsem.at[1]),
         pltpu.make_async_copy(down_hbm, down, wsem.at[2]),
     ]
-    for c in weight_copies:
-        c.start()
-
     def at_rows(slot):
         return pl.ds(pl.multiple_of(slot * rows, rows), rows)
 
@@ -112,7 +109,7 @@
         landed(tok.at[at_half(base + jd, 0)], ag_s.at[2, s], ag_r.at[2, s], Y)
         landed(tok.at[at_half(base + jd, 1)], ag_s.at[3, s], ag_r.at[3, s], X)
 
-    gtile = tile_of(keep, 256)
+    gtile = tile_of(keep, 512)
 
     def project(s, side, put):
         here = pl.ds(pl.multiple_of(plane[s] * block, block), block)
@@ -181,32 +178,37 @@
     spread_xy(0)
     for i in range(1, LINE):
         send(ext, tok.at[at_rows(me)], col_s.at[i - 1], col_r.at[z], {"dp": peers[i - 1]})
+    for c in weight_copies:
+        c.start()
     half_forward(0)
     column_forward(1)
+    half_forward(1)
+    column_forward(2)
     own_copy.wait()
-    for s in range(LINE):
+    order = list(range(1, LINE)) + [0]
+    for k, s in enumerate(order):
         diag_wait(s)
-        if s == 0:
+        if k == 0:
             weight_copies[0].wait()
             weight_copies[1].wait()
         project(s, 1 - core, psend.at[s])
         send(psend.at[s], precv.at[s], ep_s.at[0, s], ep_r.at[0, s], E)
         project(s, core, pown)
         hide(s)
-        if s + 1 < LINE:
-            half_forward(s + 1)
-        if s + 2 < LINE:
-            column_forward(s + 2)
-        if s >= 1:
-            reduce_first(s - 1)
-        if s >= 2:
-            reduce_second(s - 2)
-        if s == 0:
+        if k + 2 < LINE:
+            half_forward(k + 2)
+        if k + 3 < LINE:
+            column_forward(k + 3)
+        if k >= 1:
+            reduce_first(order[k - 1])
+        if k >= 2:
+            reduce_second(order[k - 2])
+        if k == 0:
             weight_copies[2].wait()
         lower(s)
-    reduce_first(LINE - 1)
-    reduce_second(LINE - 2)
-    reduce_second(LINE - 1)
+    reduce_first(order[-1])
+    reduce_second(order[-2])
+    reduce_second(order[-1])
     total = acc[...]
     for s in range(1, LINE):
         landed(zland.at[plane[s]], z_s.at[s], z_r.at[plane[s]], X)

time: 95.5 us -> 87.8 us (0.919)
  Pallas kernels: 90.2 us -> 82.5 us
    pallas_call x1, Pallas kernels: 90.2 us -> 82.5 us  [fused(): pl.pallas_call(functools.partial(kernel, groups), out_shape=jax.ShapeDtyp...]
where the time goes in v3:
time: 87.8 us; the launch traced here: 87.5 us
  Pallas kernels  82.5 us (94%)
  local copies, waits for them, and re-layouts  3.5 us (4%)
  other arithmetic  1.51 us (2%)
    pallas_call x1, Pallas kernels, fused(): pl.pallas_call(functools.partial(kernel, groups), out_shape=jax.ShapeDtyp...  82.5 us

profile of v3, /device:TPU:0, one launch (start us, length us, event | category | flops | bytes accessed | tf_op | source)
XLA Modules:
  0.0 87.5 jit_solution(758076351555829173)
XLA Ops:
  0.0 0.8 select_reduce_fusion.1
  0.8 0.7 select_reduce_fusion
  1.5 0.1 copy.13
  1.6 0.1 copy.12
  1.7 1.7 %concatenate.3.ext = bf16[32,3712]{1,0:T(8,128)(2,1)} concatenate(bf16[32,3584]{1,0:T(8,128)(2,1)} %param.7, bf16[32,16]{1,0:T(8,128)(2,1)S(1)} %get-tuple-element.7, bf16[32,16]{1,0:T(8,128)(2,1)S(1)} %get-tuple-element.6, bf16[32,16]{1,0:T(8,128)(2,1)S(1)} %get-tuple-element.5, bf16[32,80]{1,0:T(8,128)(2,1)S(1)} %broadcast_in_dim.37), dimensions={1} | concatenate | bytes 475136 | tf_op jit(solution)/shard_map/concatenate | solution.py:230
  3.4 82.5 %shard_map.73 = bf16[32,3584]{1,0:T(8,128)(2,1)} custom-call(bf16[32,3712]{1,0:T(8,128)(2,1)} %concatenate.3.ext, bf16[3584,1024]{1,0:T(8,128)(2,1)} %bitcast.3, bf16[3584,1024]{1,0:T(8,128)(2,1)} %bitcast.4, bf16[1024,3584]{1,0:T(8,128)(2,1)} %bitcast.5), custom_call_target="tpu_custom_call" | custom-call | tf_op jit(solution)/shard_map/pallas_call | solution.py:238
  85.9 1.6 %copy.16 = bf16[32,3584]{1,0:T(8,128)(2,1)} copy(bf16[32,3584]{1,0:T(8,128)(2,1)} %shard_map.73) | data formatting | bytes 458752
  (3 shorter events, 0.0 us)

commit v4 on v3

--- a/solution.py
+++ b/solution.py
@@ -150,24 +150,28 @@
         dsend[s] = cont[s, at_rows(jd)].astype(BF16)
         send(dsend.at[s, pl.ds(0, half)], dland.at[s, pl.ds(0, half)], rs_s.at[0, s], rs_r.at[0, s], Y)
         send(dsend.at[s, pl.ds(half, half)], dland.at[s, pl.ds(half, half)], rs_s.at[1, s], rs_r.at[1, s], X)
+        xsend[s, pl.ds(half, half)] = cont[s, at_half(jx, 1)].astype(BF16)
+        send(xsend.at[s, pl.ds(half, half)], xland.at[s, pl.ds(half, half)], rs_s.at[4, s], rs_r.at[4, s], X)
+        ysend[s, pl.ds(0, half)] = cont[s, at_half(jy, 0)].astype(BF16)
+        send(ysend.at[s, pl.ds(0, half)], yland.at[s, pl.ds(0, half)], rs_s.at[5, s], rs_r.at[5, s], Y)
 
     def reduce_first(s):
         landed(dland.at[s, pl.ds(0, half)], rs_s.at[0, s], rs_r.at[0, s], Y)
         xsend[s, pl.ds(0, half)] = (
             cont[s, at_half(jx, 0)] + dland[s, pl.ds(0, half)].astype(F32)
         ).astype(BF16)
-        xsend[s, pl.ds(half, half)] = cont[s, at_half(jx, 1)].astype(BF16)
-        send(xsend.at[s], xland.at[s], rs_s.at[2, s], rs_r.at[2, s], X)
+        send(xsend.at[s, pl.ds(0, half)], xland.at[s, pl.ds(0, half)], rs_s.at[2, s], rs_r.at[2, s], X)
         landed(dland.at[s, pl.ds(half, half)], rs_s.at[1, s], rs_r.at[1, s], X)
-        ysend[s, pl.ds(0, half)] = cont[s, at_half(jy, 0)].astype(BF16)
         ysend[s, pl.ds(half, half)] = (
             cont[s, at_half(jy, 1)] + dland[s, pl.ds(half, half)].astype(F32)
         ).astype(BF16)
-        send(ysend.at[s], yland.at[s], rs_s.at[3, s], rs_r.at[3, s], Y)
+        send(ysend.at[s, pl.ds(half, half)], yland.at[s, pl.ds(half, half)], rs_s.at[3, s], rs_r.at[3, s], Y)
 
     def reduce_second(s):
-        landed(xland.at[s], rs_s.at[2, s], rs_r.at[2, s], X)
-        landed(yland.at[s], rs_s.at[3, s], rs_r.at[3, s], Y)
+        landed(xland.at[s, pl.ds(half, half)], rs_s.at[4, s], rs_r.at[4, s], X)
+        landed(yland.at[s, pl.ds(0, half)], rs_s.at[5, s], rs_r.at[5, s], Y)
+        landed(xland.at[s, pl.ds(0, half)], rs_s.at[2, s], rs_r.at[2, s], X)
+        landed(yland.at[s, pl.ds(half, half)], rs_s.at[3, s], rs_r.at[3, s], Y)
         total = cont[s, at_rows(j)] + xland[s].astype(F32) + yland[s].astype(F32)
         if s == 0:
             acc[...] = total
@@ -206,8 +210,8 @@
         if k == 0:
             weight_copies[2].wait()
         lower(s)
+    reduce_second(order[-2])
     reduce_first(order[-1])
-    reduce_second(order[-2])
     reduce_second(order[-1])
     total = acc[...]
     for s in range(1, LINE):
@@ -253,7 +257,7 @@
             VM((rows, wide), F32),
             DMA((3,)), DMA((1,)), DMA((LINE - 1,)), DMA((LINE,)),
             DMA((4, LINE)), DMA((4, LINE)), DMA((2, LINE)), DMA((2, LINE)),
-            DMA((4, LINE)), DMA((4, LINE)), DMA((LINE,)), DMA((LINE,)),
+            DMA((6, LINE)), DMA((6, LINE)), DMA((LINE,)), DMA((LINE,)),
         ],
         compiler_params=pltpu.CompilerParams(
             collective_id=0, has_side_effects=True, vmem_limit_bytes=63 * 1024 * 1024

time: 87.8 us -> 88 us (level)
  no operation moved by 1% of the time
where the time goes in v4:
time: 88 us; the launch traced here: 87.7 us
  Pallas kernels  82.7 us (94%)
  local copies, waits for them, and re-layouts  3.5 us (4%)
  other arithmetic  1.51 us (2%)
    pallas_call x1, Pallas kernels, fused(): pl.pallas_call(functools.partial(kernel, groups), out_shape=jax.ShapeDtyp...  82.7 us

profile of v4, /device:TPU:0, one launch (start us, length us, event | category | flops | bytes accessed | tf_op | source)
XLA Modules:
  0.0 87.7 jit_solution(14325121583617443665)
XLA Ops:
  0.0 0.8 select_reduce_fusion.1
  0.8 0.7 select_reduce_fusion
  1.5 0.1 copy.13
  1.6 0.1 copy.12
  1.7 1.7 %concatenate.3.ext = bf16[32,3712]{1,0:T(8,128)(2,1)} concatenate(bf16[32,3584]{1,0:T(8,128)(2,1)} %param.7, bf16[32,16]{1,0:T(8,128)(2,1)S(1)} %get-tuple-element.7, bf16[32,16]{1,0:T(8,128)(2,1)S(1)} %get-tuple-element.6, bf16[32,16]{1,0:T(8,128)(2,1)S(1)} %get-tuple-element.5, bf16[32,80]{1,0:T(8,128)(2,1)S(1)} %broadcast_in_dim.37), dimensions={1} | concatenate | bytes 475136 | tf_op jit(solution)/shard_map/concatenate | solution.py:234
  3.4 82.7 %shard_map.73 = bf16[32,3584]{1,0:T(8,128)(2,1)} custom-call(bf16[32,3712]{1,0:T(8,128)(2,1)} %concatenate.3.ext, bf16[3584,1024]{1,0:T(8,128)(2,1)} %bitcast.3, bf16[3584,1024]{1,0:T(8,128)(2,1)} %bitcast.4, bf16[1024,3584]{1,0:T(8,128)(2,1)} %bitcast.5), custom_call_target="tpu_custom_call" | custom-call | tf_op jit(solution)/shard_map/pallas_call | solution.py:242
  86.1 1.6 %copy.16 = bf16[32,3584]{1,0:T(8,128)(2,1)} copy(bf16[32,3584]{1,0:T(8,128)(2,1)} %shard_map.73) | data formatting | bytes 458752
  (3 shorter events, 0.0 us)
